TPU v7x, 512 devices: a whole 4x4x16 slice. The times are simulated.
512 devices in a mesh: tm: 64 (over y, z), head: 8 (over x, core).
Axes of the slice: x: 4, y: 4, z: 16, core: 2. Of those that a mesh axis runs over, the one named last changes fastest.
Arguments:
- frames: bfloat16 [16384, 1024], P('tm'), may hold values from -6 to 6
- x_weight: bfloat16 [1024, 2048], P('tm', 'head'), may hold values from -0.1875 to 0.1875
- z_weight: bfloat16 [1024, 2048], P('tm', 'head'), may hold values from -0.1875 to 0.1875
- bc_weight: bfloat16 [1024, 256], P('tm'), may hold values from -0.1875 to 0.1875
- log_decay: float32 [32, 16384], P('head', 'tm'), may hold values from -0.9 to 0
- norm_gain: float32 [2048], P('head'), may hold values from 0.1 to 1.9
- conv_weight: float32 [31, 2048], P(None, 'head'), may hold values from -1 to 1
- out_weight: bfloat16 [2048, 1024], P('head', 'tm'), may hold values from -0.125 to 0.125
- record_lengths: int32 [8], replicated, may hold values from 1 to 12288, 16384 in all
Outputs:
- mixed: bfloat16 [16384, 1024], P('tm', 'head')
Inputs may be any that keep to these rules, and one draw needn't show every extreme that they name: `record_lengths`: 8 recording lengths that sum to 16384; the longest has exactly 12288 frames.
All inputs are finite; a program needn't handle non-finite values.
Results may differ from a plain program's by a relative error of at most 0.02.
Values may be sent and summed in bfloat16 or wider, within the bound.
A program may use at most 64 MiB of HBM per device.

v0:
```python
import jax
import jax.numpy as jnp
from jax import lax
from jax.sharding import PartitionSpec as P

SPAN = 128


highest = lax.Precision.HIGHEST


def extended_2(array, sides, width):
    for axis, dim in sides:
        peers, length = (lax.axis_size(axis), array.shape[dim])
        up = [(i, (i + 1) % peers) for i in range(peers - 1)]
        down = [(j, i) for i, j in up]
        last = lax.slice_in_dim(array, length - width, length, axis=dim)
        leading = lax.slice_in_dim(array, 0, width, axis=dim)
        before = lax.ppermute(last, axis, up)
        after = lax.ppermute(leading, axis, down)
        array = jnp.concatenate([before, array, after], axis=dim)
    return array


def segment_ids(record_lengths, positions):
    record_ends = jnp.cumsum(record_lengths)
    return jnp.sum((record_ends[None, :] <= positions[:, None]).astype(jnp.int32), axis=1)


def span_step(state, inputs):
    x_block, b_block, c_block, log_block, seg_block, seg_before = inputs
    length = seg_block.shape[0]
    cumul = jnp.cumsum(log_block, axis=1)
    lower = jnp.arange(length)[:, None] >= jnp.arange(length)[None, :]
    joined = (seg_block[:, None] == seg_block[None, :]) & lower
    spread = cumul[:, :, None] - cumul[:, None, :]
    mixing = jnp.exp(jnp.where(joined[None], spread, -jnp.inf))
    scores = jnp.dot(c_block, b_block.T, preferred_element_type=jnp.float32)
    x_float = x_block.astype(jnp.float32)
    inner = jnp.einsum("hts,shp->thp", mixing * scores[None], x_float, precision=highest)
    carried = jnp.exp(cumul) * (seg_block == seg_before).astype(jnp.float32)[None, :]
    c_float = c_block.astype(jnp.float32)
    outer = jnp.einsum("tn,hnp->thp", c_float, state, precision=highest) * carried.T[:, :, None]
    tail = (
        jnp.exp(cumul[:, -1:] - cumul) * (seg_block == seg_block[-1]).astype(jnp.float32)[None, :]
    )
    weighted = tail[:, :, None] * b_block.astype(jnp.float32)[None, :, :]
    state_next = carried[:, -1][:, None, None] * state + jnp.einsum(
        "hsn,shp->hnp", weighted, x_float, precision=highest
    )
    return (state_next, inner + outer)


def run_spans(x_rows, b_rows, c_rows, log_rows, seg_rows, seg_first, state):
    count = x_rows.shape[0] // SPAN
    heads_here = log_rows.shape[0]
    x_blocks = x_rows.reshape(count, SPAN, heads_here, -1)
    b_blocks = b_rows.reshape(count, SPAN, -1)
    c_blocks = c_rows.reshape(count, SPAN, -1)
    log_blocks = log_rows.reshape(heads_here, count, SPAN).transpose(1, 0, 2)
    seg_blocks = seg_rows.reshape(count, SPAN)
    seg_befores = jnp.concatenate([jnp.reshape(seg_first, (1,)), seg_blocks[:-1, -1]])
    state, outputs = lax.scan(
        span_step, state, (x_blocks, b_blocks, c_blocks, log_blocks, seg_blocks, seg_befores)
    )
    return (state, outputs.reshape(count * SPAN, heads_here, -1))


def gate_rows(ssd_out, z_rows, norm_gain):
    square_mean = jnp.mean(ssd_out * ssd_out, axis=-1, keepdims=True)
    normed = (ssd_out * lax.rsqrt(square_mean + 1e-05)).reshape(ssd_out.shape[0], -1)
    z_float = z_rows.astype(jnp.float32)
    return (normed * norm_gain[None, :] * z_float * jax.nn.sigmoid(z_float)).astype(jnp.bfloat16)


def conv_rows(extended, seg_extended, seg_rows, conv_weight):
    frame_count = seg_rows.shape[0]
    summed = jnp.zeros((frame_count, extended.shape[1]), jnp.float32)
    for offset in range(conv_weight.shape[0]):
        same = (seg_extended[offset : offset + frame_count] == seg_rows).astype(jnp.float32)
        summed = (
            summed
            + conv_weight[offset][None, :]
            * extended[offset : offset + frame_count].astype(jnp.float32)
            * same[:, None]
        )
    return (summed * jax.nn.sigmoid(summed)).astype(jnp.bfloat16)


def local(
    frames,
    x_weight,
    z_weight,
    bc_weight,
    log_decay,
    norm_gain,
    conv_weight,
    out_weight,
    record_lengths,
):
    frame_count = frames.shape[0]
    state_width = bc_weight.shape[1] // 2
    pieces = (
        lax.all_gather(x_weight, "tm", axis=0, tiled=True),
        lax.all_gather(z_weight, "tm", axis=0, tiled=True),
        lax.all_gather(bc_weight, "tm", axis=0, tiled=True),
    )
    x_sum, z_sum, bc_sum = tuple(
        (jnp.dot(frames, weight_rows, preferred_element_type=jnp.float32) for weight_rows in pieces)
    )
    bc_rows = bc_sum.astype(jnp.bfloat16)
    x_rows = x_sum.astype(jnp.bfloat16)
    z_rows = z_sum.astype(jnp.bfloat16)
    dev_start = lax.axis_index("tm") * frame_count
    positions = dev_start + jnp.arange(frame_count, dtype=jnp.int32)
    seg_rows = segment_ids(record_lengths, positions)
    seg_before_dev = segment_ids(record_lengths, jnp.reshape(dev_start - 1, (1,)))[0]
    seg_first = jnp.where(dev_start == 0, -1, seg_before_dev)
    heads_here = log_decay.shape[0]
    head_size = x_weight.shape[1] // heads_here
    empty_state = jnp.zeros((heads_here, state_width, head_size), jnp.float32)
    local_state, local_out = run_spans(
        x_rows,
        bc_rows[:, :state_width],
        bc_rows[:, state_width:],
        log_decay,
        seg_rows,
        seg_first,
        empty_state,
    )
    same_first = (seg_rows == seg_first).astype(jnp.float32)
    through = jnp.exp(jnp.sum(log_decay, axis=1)) * same_first[-1]
    all_keep, all_summaries = (
        lax.all_gather(through[None], "tm", axis=0, tiled=True),
        lax.all_gather(local_state[None], "tm", axis=0, tiled=True),
    )
    dev_index = lax.axis_index("tm")

    def absorb(position, carry_state):
        updated = all_keep[position][:, None, None] * carry_state + all_summaries[position]
        return jnp.where(position < dev_index, updated, carry_state)

    entry_state = lax.fori_loop(0, all_keep.shape[0], absorb, empty_state)
    growth = jnp.exp(jnp.cumsum(log_decay, axis=1)) * same_first[None, :]
    carried = (
        jnp.einsum(
            "tn,hnp->thp",
            bc_rows[:, state_width:].astype(jnp.float32),
            entry_state,
            precision=highest,
        )
        * growth.T[:, :, None]
    )
    ssd_out = local_out + carried
    gated = gate_rows(ssd_out, z_rows, norm_gain)
    half_width = (conv_weight.shape[0] - 1) // 2
    extended = extended_2(gated, (("tm", 0),), half_width)
    seg_extended = segment_ids(
        record_lengths,
        dev_start - half_width + jnp.arange(frame_count + 2 * half_width, dtype=jnp.int32),
    )
    act_rows = conv_rows(extended, seg_extended, seg_rows, conv_weight)
    partial_terms = jnp.dot(
        act_rows,
        lax.all_gather(out_weight, "tm", axis=1, tiled=True),
        preferred_element_type=jnp.float32,
    )
    return lax.psum_scatter(
        partial_terms.astype(jnp.bfloat16), "head", scatter_dimension=1, tiled=True
    )


def solution(mesh):
    in_specs = (
        P("tm", None),
        P("tm", "head"),
        P("tm", "head"),
        P("tm", None),
        P("head", "tm"),
        P("head"),
        P(None, "head"),
        P("head", "tm"),
        P(),
    )
    out_specs = P("tm", "head")
    return jax.shard_map(local, mesh=mesh, in_specs=in_specs, out_specs=out_specs, check_vma=False)
```

profile of v0, /device:TPU:1, one launch (start us, length us, event | category | flops | bytes accessed | tf_op | source)
XLA Modules:
  0.0 708.1 jit_solution(988738983611834852)
XLA Ops:
  8.9 81.9 %all_gather.18 = bf16[1024,256]{1,0:T(8,128)(2,1)S(1)} all-gather(bf16[16,256]{1,0:T(8,128)(2,1)} %param.16), channel_id=1, replica_groups=mesh['tm'=64,'head'=8] {'tm'}, dimensions={0}, use_global_device_ids=true | all-gather | bytes 532480 | tf_op jit(solution)/shard_map/all_gather | solution.py:106
  91.1 73.5 %all_gather.19 = bf16[1024,256]{1,0:T(8,128)(2,1)S(1)} all-gather(bf16[16,256]{1,0:T(8,128)(2,1)} %param.14), channel_id=1, replica_groups=mesh['tm'=64,'head'=8] {'tm'}, dimensions={0}, use_global_device_ids=true | all-gather | bytes 532480 | tf_op jit(solution)/shard_map/all_gather | solution.py:104
  166.7 16.3 %while.27 = (s32[]{:T(128)}, f32[4,128,64]{1,2,0:T(8,128)S(1)}, f32[2,128,4,64]{1,0,3,2:T(2,128)S(1)}, f32[2,4,128]{2,1,0:T(4,128)}, s32[2,128]{1,0:T(2,128)S(1)...) while((s32[]{:T(128)}, f32[4,128,64]{1,2,0:T(8,128)S(1)}, ...), condition=%wide.region_5.6_spmd.clone, body=%wide.region_3.5_spmd.clone.sunk | while | flops 155747840 | bytes 1896203 | solution.py:63
  171.7 2.6 dynamic_update_slice.6
  179.9 2.6 dynamic_update_slice.6
  185.4 1.3 dynamic-slice
  188.2 112.5 %all-reduce = f32[256]{0:T(256)S(1)} all-reduce(f32[256]{0:T(256)S(1)} %multiply_dynamic-update-slice_fusion), channel_id=2, replica_groups=mesh['tm'=64,'head'=8] {'tm'}, use_global_device_ids=true, to_apply=%add | all-reduce | flops 256 | bytes 2048
  301.5 1.2 reduce-window.11
  303.3 79.7 %all_gather.22 = bf16[1024,256]{1,0:T(8,128)(2,1)S(1)} all-gather(bf16[16,256]{1,0:T(8,128)(2,1)S(1)} %copy-done.3), channel_id=1, replica_groups=mesh['tm'=64,'head'=8] {'tm'}, dimensions={0}, use_global_device_ids=true | all-gather | bytes 532480 | tf_op jit(solution)/shard_map/all_gather | solution.py:105
  383.3 77.0 %while.28 = (s32[]{:T(128)}, f32[4,128,64]{2,1,0:T(8,128)S(1)}, s32[]{:T(128)}, f32[64,4]{1,0:T(8,128)S(1)}, f32[64,4,128,64]{2,3,1,0:T(8,128)}, /*index=5*/s32[]{:T(128)}, s32[]{:T(128)}) while((s32[]{:T(128)}, f32[4,128,64]{2,1,0:T(8,128)S(1)}, s32[]{:T(128)}, f32[64,4]{1,0:T(8,128)S(1)}, f32[64,4,128,64]{2,3,1,0:T(8,128)}, ...), condition=%wide.region_8.9_spmd.clone, body=%wide.region_7.8_spmd.clone.sunk | while | flops 131076 | bytes 917657 | solution.py:143
  383.3 0.9 constant_dynamic-slice_fusion.4
  384.5 0.9 constant_dynamic-slice_fusion.4
  385.7 0.9 constant_dynamic-slice_fusion.4
  390.5 0.9 constant_dynamic-slice_fusion.4
  391.7 0.9 constant_dynamic-slice_fusion.4
  392.9 0.9 constant_dynamic-slice_fusion.4
  394.1 0.9 constant_dynamic-slice_fusion.4
  395.3 0.9 constant_dynamic-slice_fusion.4
  396.5 0.9 constant_dynamic-slice_fusion.4
  397.7 0.9 constant_dynamic-slice_fusion.4
  401.3 0.9 constant_dynamic-slice_fusion.4
  402.5 0.9 constant_dynamic-slice_fusion.4
  403.7 0.9 constant_dynamic-slice_fusion.4
  404.9 0.9 constant_dynamic-slice_fusion.4
  406.1 0.9 constant_dynamic-slice_fusion.4
  407.3 0.9 constant_dynamic-slice_fusion.4
  408.5 0.9 constant_dynamic-slice_fusion.4
  413.3 0.9 constant_dynamic-slice_fusion.4
  414.6 0.9 constant_dynamic-slice_fusion.4
  415.8 0.9 constant_dynamic-slice_fusion.4
  417.0 0.9 constant_dynamic-slice_fusion.4
  418.2 0.9 constant_dynamic-slice_fusion.4
  419.4 0.9 constant_dynamic-slice_fusion.4
  420.6 0.9 constant_dynamic-slice_fusion.4
  424.2 0.9 constant_dynamic-slice_fusion.4
  425.4 0.9 constant_dynamic-slice_fusion.4
  426.6 0.9 constant_dynamic-slice_fusion.4
  427.8 0.9 constant_dynamic-slice_fusion.4
  429.0 0.9 constant_dynamic-slice_fusion.4
  430.2 0.9 constant_dynamic-slice_fusion.4
  431.4 0.9 constant_dynamic-slice_fusion.4
  461.2 3.7 collective-permute-start
  464.9 1.3 collective-permute-start.1
  466.2 75.3 %all_gather.23 = bf16[256,1024]{0,1:T(8,128)(2,1)S(1)} all-gather(bf16[256,16]{0,1:T(8,128)(2,1)S(1)} %copy-done.4), channel_id=1, replica_groups=mesh['tm'=64,'head'=8] {'tm'}, dimensions={1}, use_global_device_ids=true | all-gather | bytes 532480 | tf_op jit(solution)/shard_map/all_gather | solution.py:165
  541.6 3.0 convolution_convert_fusion
  544.6 1.0 copy.47
  545.6 154.0 %reduce-scatter.4.cloned.1.call-done = bf16[128,256]{1,0:T(8,128)(2,1)} async-done(((bf16[1024,256]{1,0:T(8,128)(2,1)}), bf16[128,256]{1,0:T(8,128)(2,1)}) %reduce-scatter.4.cloned.1.call-update) | async-done | bytes 65552
  699.6 1.6 copy.48
  (317 shorter events, 66.2 us)
Async XLA Ops:
  6.5 84.3 %copy-start = (bf16[256,1024]{1,0:T(8,128)(2,1)S(1)}, bf16[256,1024]{1,0:T(8,128)(2,1)}, u32[]{:S(2)}) copy-start(bf16[256,1024]{1,0:T(8,128)(2,1)} %param.13) | copy-start | bytes 1572868
  6.5 296.7 %copy-start.3 = (bf16[16,256]{1,0:T(8,128)(2,1)S(1)}, bf16[16,256]{1,0:T(8,128)(2,1)}, u32[]{:S(2)}) copy-start(bf16[16,256]{1,0:T(8,128)(2,1)} %param.15) | copy-start | bytes 24580
  6.5 376.5 %copy-start.2 = (f32[31,256]{1,0:T(8,128)S(1)}, f32[31,256]{1,0:T(8,128)}, u32[]{:S(2)}) copy-start(f32[31,256]{1,0:T(8,128)} %param.19) | copy-start | bytes 95236
  6.5 376.7 %all-gather.4.cloned.1.call-start = ((), (), s32[]{:S(2)}) async-start(), calls=%async_computation.1 | async-start | bytes 8519680 | tf_op jit(solution)/shard_map/all_gather | solution.py:135
  166.7 294.2 %copy-start.5 = (f32[256]{0:T(256)S(1)}, f32[256]{0:T(256)}, u32[]{:S(2)}) copy-start(f32[256]{0:T(256)} %param.18) | copy-start | bytes 3076
  183.0 0.7 copy-start.1
  183.1 283.2 %copy-start.4 = (bf16[256,16]{0,1:T(8,128)(2,1)S(1)}, bf16[256,16]{0,1:T(8,128)(2,1)}, u32[]{:S(2)}) copy-start(bf16[256,16]{0,1:T(8,128)(2,1)} %param.20) | copy-start | bytes 24580
  183.7 515.9 %reduce-scatter.4.cloned.1.call-start = ((), (), s32[]{:S(2)}) async-start(), calls=%async_computation.2 | async-start | bytes 589824
  461.2 80.3 %collective-permute-start = (bf16[15,256]{1,0:T(8,128)(2,1)S(1)}, bf16[15,256]{1,0:T(8,128)(2,1)S(1)}, u32[]{:S(2)}, u32[]{:S(2)}) collective-permute-start(bf16[15,256]{1,0:T(8,128)(2,1)S(1)} %get-tuple-element.276), channel_id=1, source_target_pairs={{0,8},{8,16},{16,24},{24,32},{32,40},{40,48},{48,56},{56,64},{64,7... | collective-permute-start | bytes 23048 | tf_op jit(solution)/shard_map/ppermute | solution.py:19
  464.9 76.6 %collective-permute-start.1 = (bf16[15,256]{1,0:T(8,128)(2,1)S(1)}, bf16[15,256]{1,0:T(8,128)(2,1)S(1)}, u32[]{:S(2)}, u32[]{:S(2)}) collective-permute-start(bf16[15,256]{1,0:T(8,128)(2,1)S(1)} %get-tuple-element.277), channel_id=1, source_target_pairs={{8,0},{16,8},{24,16},{32,24},{40,32},{48,40},{56,48},{64,56},{72,6... | collective-permute-start | bytes 23048 | tf_op jit(solution)/shard_map/ppermute | solution.py:20
Sparse Core Ops, SparseCore 0:
  183.8 195.2 all-gather.3
  545.7 153.8 reduce-scatter.3
where the time goes:
time: 710 us; the launch traced here: 708 us
  blocking collectives  423 us (60%)
  waiting for transfers between devices  154 us (22%)
  local copies, waits for them, and re-layouts  85.5 us (12%)
  other arithmetic  15.8 us (2%)
  between operations  15 us (2%)
    unnamed x3, waiting for transfers between devices  154 us
    unnamed x1, blocking collectives  113 us
    all_gather x1, blocking collectives, local(): lax.all_gather(bc_weight, 'tm', axis=0, tiled=True)  81.9 us
    all_gather x1, blocking collectives, local(): lax.all_gather(z_weight, 'tm', axis=0, tiled=True)  79.7 us
    all_gather x1, blocking collectives, local(): lax.all_gather(out_weight, 'tm', axis=1, tiled=True)  75.3 us
    all_gather x1, blocking collectives, local(): lax.all_gather(x_weight, 'tm', axis=0, tiled=True)  73.5 us
    dynamic_slice x128, local copies, waits for them, and re-layouts, absorb(): all_summaries[position]  67 us
  transfers between devices with their start and end apart: 4, of which 1 were waited for; matrix products, arithmetic and copies ran while one was open for 1% of the time, Pallas kernels for 0%

commit v1 on v0

v1 whole, which is shorter than its diff:
```python
import functools

import jax
import jax.numpy as jnp
from jax import lax
from jax.experimental import pallas as pl
from jax.experimental.pallas import tpu as pltpu
from jax.sharding import PartitionSpec as P

NY = 4
MESH = pl.DeviceIdType.MESH
HIGHEST = lax.Precision.HIGHEST
F32 = jnp.float32
BF16 = jnp.bfloat16
PS = 64


def nt(a, b, **kw):
    return lax.dot_general(a, b, (((1,), (1,)), ((), ())), preferred_element_type=F32, **kw)


def tn(a, b, **kw):
    return lax.dot_general(a, b, (((0,), (0,)), ((), ())), preferred_element_type=F32, **kw)


def nn(a, b, **kw):
    return jnp.dot(a, b, preferred_element_type=F32, **kw)


def iota(shape, dim):
    return lax.broadcasted_iota(jnp.int32, shape, dim)


def kernel(
    ny, nz, nx,
    lens, frames, xw, zw, bcw, logd, gain, convw, outw, out,
    ga, gb, mix, growth, tail, wm, xs, bcs, inner, zs, local, got, keeps, keep_own,
    pref, ckeep, tot, tots, back, entry, gated, ext, halo_lo, halo_hi, act,
    part, pair, red, redin,
    s_loc, s_ay, r_ay, s_az, r_az, s_bz, r_bz, s_by, r_by,
    s_k, r_k, s_s, r_s, s_t, r_t, s_p, r_p, s_h, r_h, s_c, r_c, s_x, r_x,
):
    me, hd = lax.axis_index("tm"), lax.axis_index("head")
    y, z = lax.div(me, nz), lax.rem(me, nz)
    x, core = lax.div(hd, 2), lax.rem(hd, 2)
    rows, depth, chans = frames.shape[0], xw.shape[0], xw.shape[1]
    width = frames.shape[1]
    heads = chans // PS
    states = bcw.shape[1] // 2
    taps = convw.shape[0]
    half = (taps - 1) // 2
    far = nz // 2
    base = me * rows

    def at(yy, zz):
        return {"tm": yy * nz + zz}

    def turn(a, d, n):
        return lax.rem(a + d + n, n)

    pending = []

    def send(src, dst, ssem, rsem, dev):
        copy = pltpu.make_async_remote_copy(
            src_ref=src, dst_ref=dst, send_sem=ssem, recv_sem=rsem,
            device_id=dev, device_id_type=MESH,
        )
        copy.start()
        pending.append(copy)

    def recv(dst, rsem):
        pltpu.make_async_copy(dst, dst, rsem).wait()

    own = [
        pltpu.make_async_copy(xw, ga.at[0, y, z], s_loc.at[0]),
        pltpu.make_async_copy(bcw, ga.at[1, y, z], s_loc.at[1]),
        pltpu.make_async_copy(zw, gb.at[0, y, z], s_loc.at[2]),
    ]
    for copy in own:
        copy.start()
    barrier = pltpu.get_barrier_semaphore()
    greet = [at(turn(y, d, ny), z) for d in range(1, ny)]
    greet += [at(y, turn(z, 1, nz)), at(y, turn(z, -1, nz))]
    greet += [{"head": 2 * x + 1 - core}]
    greet += [{"head": 2 * turn(x, d, nx) + core} for d in range(1, nx)]
    for dev in greet:
        pl.semaphore_signal(barrier, inc=1, device_id=dev, device_id_type=MESH)
    eye = (iota((depth, depth), 0) == iota((depth, depth), 1)).astype(BF16)
    gb[1, y, z] = nt(eye, outw[...]).astype(BF16)
    for copy in own:
        copy.wait()
    pl.semaphore_wait(barrier, len(greet))

    def fwd_a(way, step, d):
        yy, zz = turn(y, -d, ny), turn(z, -step if way == 0 else step, nz)
        ref = ga.at[:, yy, zz]
        send(ref, ref, s_az.at[way, step, d], r_az.at[way, step + 1, d],
             at(y, turn(z, 1 if way == 0 else -1, nz)))

    def takes_a(way, step, d):
        return step < far or (step == far and (d < ny // 2) == (way == 0))

    def ref_b(way, step):
        zz = turn(z, -step if way == 0 else step, nz)
        return gb.at[:, y, zz] if step < far else gb.at[pl.ds(way, 1), y, zz]

    def fwd_b(way, step):
        zz = turn(z, -step if way == 0 else step, nz)
        ref = gb.at[:, y, zz] if step + 1 < far else gb.at[pl.ds(way, 1), y, zz]
        send(ref, ref, s_bz.at[way, step], r_bz.at[way, step + 1],
             at(y, turn(z, 1 if way == 0 else -1, nz)))

    for way in (0, 1):
        if takes_a(way, 1, 0):
            fwd_a(way, 0, 0)
    for d in range(1, ny):
        ref = ga.at[:, y, z]
        send(ref, ref, s_ay.at[d - 1], r_ay.at[d - 1], at(turn(y, d, ny), z))
    for way in (0, 1):
        fwd_b(way, 0)

    ends = []
    total = jnp.int32(0)
    for r in range(lens.shape[0]):
        total = total + lens[r]
        ends.append(total)
    pos = base + iota((rows, 1), 0)
    start = jnp.zeros((rows, 1), jnp.int32)
    for e in ends:
        start = jnp.where(pos >= e, e, start)
    stop = jnp.full((rows, 1), ends[-1], jnp.int32)
    for e in reversed(ends):
        stop = jnp.where(pos < e, e, stop)
    vals = {}

    def piece_cumul():
        low = iota((rows, rows), 0) >= iota((rows, rows), 1)
        tril = low.astype(F32)
        spread = jnp.concatenate(
            [jnp.broadcast_to(logd[h : h + 1, :], (PS, rows)) for h in range(heads)], axis=0
        )
        cum = nt(tril, spread, precision=HIGHEST)
        vals["cum"] = cum
        vals["row"] = nt(logd[...], tril, precision=HIGHEST)
        last = cum[rows - 1 : rows, :]
        last_start = start[rows - 1 : rows, :]
        growth[...] = jnp.where(start < base, jnp.exp(cum), 0.0)
        tail[...] = jnp.where(pos >= last_start, jnp.exp(last - cum), 0.0)
        keep_own[...] = jnp.where(last_start < base, jnp.exp(last), 0.0)

    def piece_mix(h):
        low = iota((rows, rows), 0) >= iota((rows, rows), 1)
        joined = low & (base + iota((rows, rows), 1) >= start)
        diff = vals["cum"][:, h * PS : h * PS + 1] - vals["row"][h : h + 1, :]
        mix[h] = jnp.exp(jnp.where(joined, diff, -1e30))

    def piece_taps(k_lo, k_hi):
        lanes = 128
        before = jnp.broadcast_to(start - pos, (rows, lanes))
        after = jnp.broadcast_to(stop - pos, (rows, lanes))
        for k in range(k_lo, k_hi):
            ok = (k - half >= before) if k <= half else (k - half < after)
            for lo in range(0, chans, lanes):
                wm[k, :, lo : lo + lanes] = jnp.where(ok, convw[k : k + 1, lo : lo + lanes], 0.0)

    pieces = [piece_cumul]
    pieces += [functools.partial(piece_mix, h) for h in range(heads)]
    pieces += [
        functools.partial(piece_taps, k, min(k + 4, taps)) for k in range(0, taps, 4)
    ]
    pieces[0]()
    pieces.pop(0)
    per_step = -(-len(pieces) // far)

    for d in range(1, ny):
        recv(ga.at[:, turn(y, -d, ny), z], r_ay.at[d - 1])
        for way in (0, 1):
            if takes_a(way, 1, d):
                fwd_a(way, 0, d)
    for step in range(1, far + 1):
        for piece in pieces[:per_step]:
            piece()
        pieces = pieces[per_step:]
        for d in range(ny):
            for way in (0, 1):
                if takes_a(way, step, d):
                    zz = turn(z, -step if way == 0 else step, nz)
                    recv(ga.at[:, turn(y, -d, ny), zz], r_az.at[way, step, d])
                    if takes_a(way, step + 1, d):
                        fwd_a(way, step, d)
        for way in (0, 1):
            recv(ref_b(way, step), r_bz.at[way, step])
            if step < far:
                fwd_b(way, step)

    for plane in (0, 1):
        for d in range(1, ny):
            ref = gb.at[plane, y]
            send(ref, ref, s_by.at[plane, d - 1], r_by.at[plane, d - 1], at(turn(y, d, ny), z))

    keeps[z] = keep_own[...]
    for d in range(1, nz):
        send(keep_own, keeps.at[z], s_k.at[d], r_k.at[d], at(y, turn(z, d, nz)))

    bc = nn(frames[...], ga[1].reshape(width, chans)).astype(BF16)
    bcs[...] = bc
    xr = nn(frames[...], ga[0].reshape(width, chans))
    xb = xr.astype(BF16)
    xs[...] = xb
    weighted = (xb.astype(F32) * tail[...]).astype(BF16)
    state = tn(bcs[:, :states], weighted).astype(BF16)
    share = local.shape[1]
    for lo in range(0, chans // 128):
        local[lo * (nz * 128 // chans) : (lo + 1) * (nz * 128 // chans)] = state[
            :, lo * 128 : lo * 128 + 128
        ].reshape(nz * 128 // chans, share, 128)
    for d in range(1, nz):
        zz = turn(z, d, nz)
        send(local.at[zz], got.at[z], s_s.at[d], r_s.at[d], at(y, zz))
    got[z] = local[z]

    scores = nt(bcs[:, states:], bcs[:, :states])
    lane_head = lax.div(iota((rows, chans), 1), PS)
    acc = jnp.zeros((rows, chans), F32)
    for h in range(heads):
        only = jnp.where(lane_head == h, xs[...].astype(F32), 0.0).astype(BF16)
        acc = acc + nn((mix[h] * scores).astype(BF16), only)
    inner[...] = acc

    for d in range(1, nz):
        zz = turn(z, -d, nz)
        recv(keeps.at[zz], r_k.at[d])
        recv(got.at[zz], r_s.at[d])
    carry = jnp.zeros((share, 128), F32)
    decay = jnp.ones((1, 128), F32)
    upper = z >= far
    for zz in range(nz):
        pref[zz] = carry
        ckeep[zz] = decay
        line = keeps[zz]
        keep = line[:, 0:128]
        for lo in range(1, chans // 128):
            keep = jnp.where(lax.div(z, nz * 128 // chans) == lo, line[:, lo * 128 : lo * 128 + 128], keep)
        carry = carry * keep + got[zz].astype(F32)
        decay = decay * keep
    tot[0:share] = carry
    tot[share : share + 8] = jnp.broadcast_to(decay, (8, 128))
    for d in range(1, ny):
        send(tot, tots.at[d - 1], s_t.at[d - 1], r_t.at[d - 1], at(turn(y, d, ny), z))
    for d in range(1, ny):
        recv(tots.at[d - 1], r_t.at[d - 1])
    come = jnp.zeros((share, 128), F32)
    for d in range(ny - 1, 0, -1):
        new = come * tots[d - 1, share : share + 1] + tots[d - 1, 0:share]
        come = jnp.where(y >= d, new, 0.0)
    for zz in range(nz):
        back[zz] = (pref[zz] + ckeep[zz] * come).astype(BF16)
    for d in range(1, nz):
        zz = turn(z, d, nz)
        send(back.at[zz], entry.at[z], s_p.at[d], r_p.at[d], at(y, zz))
    entry[z] = back[z]

    for d in range(1, ny):
        recv(gb.at[0, turn(y, -d, ny)], r_by.at[0, d - 1])
    zr = nn(frames[...], gb[0].reshape(width, chans)).astype(BF16).astype(F32)
    zs[...] = zr * jax.nn.sigmoid(zr) * gain[...]

    for d in range(1, nz):
        recv(entry.at[turn(z, -d, nz)], r_p.at[d])
    each = nz * 128 // chans
    carried = jnp.concatenate(
        [
            nn(bcs[:, states:], entry[lo * each : (lo + 1) * each].reshape(states, 128))
            for lo in range(chans // 128)
        ],
        axis=1,
    )
    ssd = inner[...] + carried * growth[...]
    same = lax.div(iota((chans, chans), 0), PS) == lax.div(iota((chans, chans), 1), PS)
    mean = nn((ssd * ssd).astype(BF16), jnp.where(same, 1.0 / PS, 0.0).astype(BF16))
    g = (ssd * lax.rsqrt(mean + 1e-05) * zs[...]).astype(BF16)
    gated[...] = g
    tms = ny * nz
    send(gated.at[pl.ds(rows - 16, 16)], halo_lo, s_h.at[0], r_h.at[0], {"tm": turn(me, 1, tms)})
    send(gated.at[pl.ds(0, 16)], halo_hi, s_h.at[1], r_h.at[1], {"tm": turn(me, -1, tms)})
    ext[16 : 16 + rows] = g.astype(F32)

    def conv(lo, hi):
        acc = jnp.zeros((hi - lo, chans), F32)
        for k in range(taps):
            off = 16 - half + k
            acc = acc + wm[k, lo:hi, :] * ext[lo + off : hi + off, :]
        act[lo:hi] = (acc * jax.nn.sigmoid(acc)).astype(BF16)

    for lo in range(16, rows - 16, 32):
        conv(lo, min(lo + 32, rows - 16))
    recv(halo_lo, r_h.at[0])
    recv(halo_hi, r_h.at[1])
    ext[0:16] = halo_lo[...].astype(F32)
    ext[16 + rows : 32 + rows] = halo_hi[...].astype(F32)
    conv(0, 16)
    conv(rows - 16, rows)

    for d in range(1, ny):
        recv(gb.at[1, turn(y, -d, ny)], r_by.at[1, d - 1])
    cols = width // (2 * nx)
    per = depth
    for j in range(2 * nx):
        ww = gb[1].reshape(width, chans)[j * cols : (j + 1) * cols]
        part[j // 2, j % 2] = nt(act[...], ww).astype(BF16)
    send(part.at[:, 1 - core], pair, s_c.at[0], r_c.at[0], {"head": 2 * x + 1 - core})
    recv(pair, r_c.at[0])
    for d in range(nx - 1, 0, -1):
        xx = turn(x, d, nx)
        red[d - 1] = (part[xx, core].astype(F32) + pair[xx].astype(F32)).astype(BF16)
        send(red.at[d - 1], redin.at[d - 1], s_x.at[d - 1], r_x.at[d - 1], {"head": 2 * xx + core})
    res = part[x, core].astype(F32) + pair[x].astype(F32)
    for d in range(1, nx):
        recv(redin.at[d - 1], r_x.at[d - 1])
        res = res + redin[d - 1].astype(F32)
    out[...] = res.astype(BF16)
    for copy in pending:
        copy.wait_send()


def solution(mesh):
    tms, groups = mesh.shape["tm"], mesh.shape["head"]
    ny, nz, nx = NY, tms // NY, groups // 2

    def local(frames, xw, zw, bcw, logd, gain, convw, outw, lens):
        rows, width = frames.shape
        depth, chans = xw.shape
        states = bcw.shape[1] // 2
        heads = logd.shape[0]
        taps = convw.shape[0]
        share = states * chans // (nz * 128)
        cols = width // groups
        dma = pltpu.SemaphoreType.DMA
        v = pltpu.VMEM
        far = nz // 2
        scratch = [
            v((2, ny, nz, depth, chans), BF16),
            v((2, ny, nz, depth, chans), BF16),
            v((heads, rows, rows), F32),
            v((rows, chans), F32),
            v((rows, chans), F32),
            v((taps, rows, chans), F32),
            v((rows, chans), BF16),
            v((rows, 2 * states), BF16),
            v((rows, chans), F32),
            v((rows, chans), F32),
            v((nz, share, 128), BF16),
            v((nz, share, 128), BF16),
            v((nz, 1, chans), F32),
            v((1, chans), F32),
            v((nz, share, 128), F32),
            v((nz, 1, 128), F32),
            v((share + 8, 128), F32),
            v((ny - 1, share + 8, 128), F32),
            v((nz, share, 128), BF16),
            v((nz, share, 128), BF16),
            v((rows, chans), BF16),
            v((rows + 32, chans), F32),
            v((16, chans), BF16),
            v((16, chans), BF16),
            v((rows, chans), BF16),
            v((nx, 2, rows, cols), BF16),
            v((nx, rows, cols), BF16),
            v((max(nx - 1, 1), rows, cols), BF16),
            v((max(nx - 1, 1), rows, cols), BF16),
            dma((3,)),
            dma((ny - 1,)), dma((ny - 1,)),
            dma((2, far + 1, ny)), dma((2, far + 1, ny)),
            dma((2, far + 1)), dma((2, far + 1)),
            dma((2, ny - 1)), dma((2, ny - 1)),
            dma((nz,)), dma((nz,)),
            dma((nz,)), dma((nz,)),
            dma((ny - 1,)), dma((ny - 1,)),
            dma((nz,)), dma((nz,)),
            dma((2,)), dma((2,)),
            dma((1,)), dma((1,)),
            dma((max(nx - 1, 1),)), dma((max(nx - 1, 1),)),
        ]
        vm = pl.BlockSpec(memory_space=pltpu.VMEM)
        return pl.pallas_call(
            functools.partial(kernel, ny, nz, nx),
            out_shape=jax.ShapeDtypeStruct((rows, cols), BF16),
            in_specs=[pl.BlockSpec(memory_space=pltpu.SMEM)] + [vm] * 8,
            out_specs=vm,
            scratch_shapes=scratch,
            compiler_params=pltpu.CompilerParams(
                collective_id=0, has_side_effects=True, vmem_limit_bytes=60 * 2**20
            ),
            name="mixer",
        )(lens, frames, xw, zw, bcw, logd, gain.reshape(1, chans), convw, outw)

    in_specs = (
        P("tm", None), P("tm", "head"), P("tm", "head"), P("tm", None), P("head", "tm"),
        P("head"), P(None, "head"), P("head", "tm"), P(),
    )
    return jax.shard_map(
        local, mesh=mesh, in_specs=in_specs, out_specs=P("tm", "head"), check_vma=False
    )
```

time: 710 us -> 81.9 us (0.12)
  blocking collectives: 423 us -> 0 us
  waiting for transfers between devices: 154 us -> 0 us
  local copies, waits for them, and re-layouts: 85.5 us -> 2.9 us
  Pallas kernels: 0 us -> 78.8 us
  other arithmetic: 15.8 us -> 0 us
  between operations: 15 us -> 0.01 us
    all_gather x4 -> x0, blocking collectives: 310 us -> none  [the longest x1 81.9 us: local(): lax.all_gather(bc_weight, 'tm', axis=0, tiled=True)]
    unnamed x3 -> x0, waiting for transfers between devices: 154 us -> none
    unnamed x1 -> x0, blocking collectives: 113 us -> none
    pallas_call x0 -> x1, Pallas kernels: none -> 78.8 us  [local(): pl.pallas_call(functools.partial(kernel, ny, nz, nx), out_shape=jax.Shape...]
    dynamic_slice x130 -> x0, local copies, waits for them, and re-layouts: 68.3 us -> none  [the longest x128 67 us: absorb(): all_summaries[position]]
  transfers between devices with their start and end apart: 4 -> 0, of which waited for: 1 -> 0; matrix products, arithmetic and copies ran while one was open for 1% -> 0% of each run, Pallas kernels for 0% -> 0%
where the time goes in v1:
time: 81.9 us; the launch traced here: 81.7 us
  Pallas kernels  78.8 us (96%)
  local copies, waits for them, and re-layouts  2.9 us (4%)
    pallas_call x1, Pallas kernels, local(): pl.pallas_call(functools.partial(kernel, ny, nz, nx), out_shape=jax.Shape...  78.8 us
    unnamed x2, local copies, waits for them, and re-layouts  2.9 us

profile of v1, /device:TPU:1, one launch (start us, length us, event | category | flops | bytes accessed | tf_op | source)
XLA Modules:
  0.0 81.7 jit_solution(7647639824852885998)
XLA Ops:
  0.0 1.4 %copy.10.outw = bf16[256,16]{1,0:T(8,128)(2,1)} copy(bf16[256,16]{0,1:T(8,128)(2,1)} %param.16) | data formatting | bytes 16384 | tf_op args[7]
  1.4 78.8 %mixer.1 = bf16[256,128]{1,0:T(8,128)(2,1)} custom-call(s32[8]{0:T(128)} %lens.1, bf16[256,1024]{1,0:T(8,128)(2,1)} %frames.1, bf16[16,256]{1,0:T(8,128)(2,1)} %xw.1, bf16[16,256]{1,0:T(8,128)(2,1)} %zw.1, bf16[16,256]{1,0:T(8,128)(2,1)} %bcw.1, f32[4,256]{1,0:T(4,128)} %logd.1, f32[1,256]{1,0:T(1,128)} %bitcast.1, f32[31,256]{1,0:T(8,128)} %convw.1, ...), custom_call_target="tpu_custom_call" | custom-call | tf_op jit(solution)/shard_map/mixer/pallas_call | solution.py:385
  80.2 1.5 %copy.12 = bf16[256,128]{1,0:T(8,128)(2,1)} copy(bf16[256,128]{1,0:T(8,128)(2,1)} %mixer.1) | data formatting | bytes 131072

commit v2 on v1

v2 whole, which is shorter than its diff:
```python
import functools

import jax
import jax.numpy as jnp
from jax import lax
from jax.experimental import pallas as pl
from jax.experimental.pallas import tpu as pltpu
from jax.sharding import PartitionSpec as P

NY = 4
EDGE = 16
MESH = pl.DeviceIdType.MESH
HIGHEST = lax.Precision.HIGHEST
F32 = jnp.float32
BF16 = jnp.bfloat16
PS = 64


def nt(a, b, **kw):
    return lax.dot_general(a, b, (((1,), (1,)), ((), ())), preferred_element_type=F32, **kw)


def tn(a, b, **kw):
    return lax.dot_general(a, b, (((0,), (0,)), ((), ())), preferred_element_type=F32, **kw)


def nn(a, b, **kw):
    return jnp.dot(a, b, preferred_element_type=F32, **kw)


def iota(shape, dim):
    return lax.broadcasted_iota(jnp.int32, shape, dim)


def kernel(
    ny, nz, nx, parts,
    lens, frames_in, xw, zw, bcw, logd_in, gain_in, convw_in, outw, out,
    w, frames, logd, gain, convw, mix, growth, tail, wm, xs, bs, cs, inner, zs,
    local, got, keeps, keep_own, pref, ckeep, tot, tots, back, entry, ext, act,
    part, pair, red, redin,
    s_loc, s_a1, r_a1, s_a2, r_a2, s_ay, r_ay, s_b1, r_b1, s_b2, r_b2, s_by, r_by,
    s_f, r_f, s_l, r_l, s_k, r_k, s_s, r_s, s_t, r_t, s_p, r_p, s_c, r_c, s_x, r_x,
):
    me, hd = lax.axis_index("tm"), lax.axis_index("head")
    y, z = lax.div(me, nz), lax.rem(me, nz)
    x, core = lax.div(hd, 2), lax.rem(hd, 2)
    tms = ny * nz
    rows, width = frames_in.shape
    depth, chans = xw.shape
    wide = rows + 2 * EDGE
    heads = chans // PS
    states = bcw.shape[1] // 2
    taps = convw_in.shape[0]
    half = (taps - 1) // 2
    reach = nz // 4
    base = me * rows
    first = base - EDGE

    def at(yy, zz):
        return {"tm": yy * nz + zz}

    def turn(a, d, n):
        return lax.rem(a + d + n, n)

    pending = []

    def send(src, dst, ssem, rsem, dev):
        copy = pltpu.make_async_remote_copy(
            src_ref=src, dst_ref=dst, send_sem=ssem, recv_sem=rsem,
            device_id=dev, device_id_type=MESH,
        )
        copy.start()
        pending.append(copy)

    def recv(dst, rsem):
        pltpu.make_async_copy(dst, dst, rsem).wait()

    barrier = pltpu.get_barrier_semaphore()
    greet = [at(y, turn(z, s * k, nz)) for k in range(reach, 0, -1) for s in (1, -1)]
    greet += [at(turn(y, d, ny), z) for d in range(1, ny)]
    greet += [{"tm": turn(me, 1, tms)}, {"tm": turn(me, -1, tms)}]
    greet += [{"head": 2 * turn(x, d, nx) + core} for d in range(1, nx)]
    greet += [{"head": 2 * x + 1 - core}]
    for dev in greet:
        pl.semaphore_signal(barrier, inc=1, device_id=dev, device_id_type=MESH)

    tiles = [(xw, 0), (xw, 128), (bcw, 0), (bcw, 128), (zw, 0), (zw, 128), (outw, 0), (outw, 128)]
    own = [
        pltpu.make_async_copy(src.at[:, lo : lo + 128], w.at[y, z, i], s_loc.at[i])
        for i, (src, lo) in enumerate(tiles)
    ]
    own.append(pltpu.make_async_copy(logd_in, logd.at[1], s_loc.at[8]))
    own.append(pltpu.make_async_copy(frames_in, frames.at[EDGE : EDGE + rows], s_loc.at[9]))
    own.append(pltpu.make_async_copy(gain_in, gain, s_loc.at[10]))
    own.append(pltpu.make_async_copy(convw_in, convw, s_loc.at[11]))
    for copy in own:
        copy.start()
    for copy in own:
        copy.wait()
    pl.semaphore_wait(barrier, len(greet))

    crit, rest = slice(0, 3), slice(3, 8)

    def stage_1(cut, ssem, rsem):
        ref = w.at[y, z, cut]
        for k in range(reach, 0, -1):
            for way, s in ((0, 1), (1, -1)):
                send(ref, ref, ssem.at[way, k], rsem.at[way, k], at(y, turn(z, s * k, nz)))

    def stage_2(cut, ssem, rsem, way):
        s = 1 - 2 * way
        ref = w.at[y, turn(z, -s * reach, nz), cut]
        for j in range(reach - way, 0, -1):
            send(ref, ref, ssem.at[way, j], rsem.at[way, j], at(y, turn(z, s * j, nz)))

    def cross(off):
        zz = turn(z, -off, nz)
        ref = w.at[y, zz, crit]
        for d in range(1, ny):
            send(ref, ref, s_ay.at[off % nz, d], r_ay.at[off % nz, d], at(turn(y, d, ny), z))

    def got_1(cut, rsem, way, k):
        recv(w.at[y, turn(z, k if way else -k, nz), cut], rsem.at[way, k])

    def got_2(cut, rsem, way, j):
        far = reach + j
        recv(w.at[y, turn(z, far if way else -far, nz), cut], rsem.at[way, j])

    stage_1(crit, s_a1, r_a1)
    cross(0)
    for i, d in enumerate((1, -1)):
        send(logd.at[1], logd.at[1 - d], s_l.at[i], r_l.at[i], {"tm": turn(me, d, tms)})
    send(frames.at[rows : rows + EDGE], frames.at[0:EDGE],
         s_f.at[0], r_f.at[0], {"tm": turn(me, 1, tms)})
    send(frames.at[EDGE : 2 * EDGE], frames.at[rows + EDGE : wide],
         s_f.at[1], r_f.at[1], {"tm": turn(me, -1, tms)})

    ends = []
    total = jnp.int32(0)
    for r in range(lens.shape[0]):
        total = total + lens[r]
        ends.append(total)

    def starts(pos):
        start = jnp.zeros(pos.shape, jnp.int32)
        for e in ends:
            start = jnp.where(pos >= e, e, start)
        return start

    pos = first + iota((wide, 1), 0)
    start = starts(pos)
    vals = {}

    def piece_cumul():
        i, j = iota((wide, rows), 0), iota((wide, rows), 1)
        cols = (
            (j >= rows - EDGE) & (j - (rows - EDGE) <= i),
            j + EDGE <= i,
            (j < EDGE) & (j + EDGE + rows <= i),
        )
        cum, line = 0.0, 0.0
        for p, col in enumerate(cols):
            ones = col.astype(F32)
            lines = logd[p]
            spread = jnp.concatenate(
                [jnp.broadcast_to(lines[h : h + 1, :], (PS, rows)) for h in range(heads)], axis=0
            )
            cum = cum + nt(ones, spread, precision=HIGHEST)
            line = line + nt(lines, ones, precision=HIGHEST)
        vals["cum"], vals["line"] = cum, line
        last = cum[rows - 1 : rows, :]
        last_start = start[rows - 1 : rows, :]
        growth[...] = jnp.where(start < first, jnp.exp(cum), 0.0)
        tail[...] = jnp.where(pos[0:rows] >= last_start, jnp.exp(last - cum[0:rows]), 0.0)
        keep_own[...] = jnp.where(last_start < first, jnp.exp(last), 0.0)

    def piece_mix(h):
        i, j = iota((wide, wide), 0), iota((wide, wide), 1)
        joined = (i >= j) & (first + j >= start)
        diff = vals["cum"][:, h * PS : h * PS + 1] - vals["line"][h : h + 1, :]
        mix[h] = jnp.exp(jnp.where(joined, diff, -1e30))

    def piece_taps(k_lo, k_hi):
        lanes = 128
        here = pos[EDGE : EDGE + rows]
        stop = jnp.full(here.shape, ends[-1], jnp.int32)
        for e in reversed(ends):
            stop = jnp.where(here < e, e, stop)
        before = jnp.broadcast_to(start[EDGE : EDGE + rows] - here, (rows, lanes))
        after = jnp.broadcast_to(stop - here, (rows, lanes))
        for k in range(k_lo, k_hi):
            ok = (k - half >= before) if k <= half else (k - half < after)
            for lo in range(0, chans, lanes):
                wm[k, :, lo : lo + lanes] = jnp.where(ok, convw[k : k + 1, lo : lo + lanes], 0.0)

    for way in (0, 1):
        got_1(crit, r_a1, way, reach)
        stage_2(crit, s_a2, r_a2, way)
    stage_1(rest, s_b1, r_b1)
    for k in range(reach, 0, -1):
        for way in (0, 1):
            if k < reach:
                got_1(crit, r_a1, way, k)
            cross(k if way == 0 else -k)
    recv(logd.at[0], r_l.at[0])
    recv(logd.at[2], r_l.at[1])
    piece_cumul()
    for j in range(1, reach + 1):
        for way in (0, 1):
            if j <= reach - way:
                got_2(crit, r_a2, way, j)
                cross(reach + j if way == 0 else -(reach + j))
    for way in (0, 1):
        got_1(rest, r_b1, way, reach)
        stage_2(rest, s_b2, r_b2, way)
    keeps[z] = keep_own[...]
    for d in range(1, nz):
        send(keep_own, keeps.at[z], s_k.at[d], r_k.at[d], at(y, turn(z, d, nz)))
    for h in range(heads):
        piece_mix(h)
    for off in range(nz):
        for d in range(1, ny):
            recv(w.at[turn(y, -d, ny), turn(z, -off, nz), crit], r_ay.at[off, d])

    recv(frames.at[0:EDGE], r_f.at[0])
    recv(frames.at[rows + EDGE : wide], r_f.at[1])

    def weight(lo, count):
        return jnp.concatenate(
            [w[:, :, lo + i].reshape(width, 128) for i in range(count)], axis=1
        )

    bs[...] = nn(frames[...], weight(2, 1)).astype(BF16)
    xb = nn(frames[...], weight(0, 2)).astype(BF16)
    xs[...] = xb
    weighted = (xb[0:rows].astype(F32) * tail[...]).astype(BF16)
    state = tn(bs[0:rows], weighted).astype(BF16)
    share = local.shape[1]
    each = nz * 128 // chans
    for lo in range(chans // 128):
        local[lo * each : (lo + 1) * each] = state[:, lo * 128 : lo * 128 + 128].reshape(
            each, share, 128
        )
    for d in range(1, nz):
        zz = turn(z, d, nz)
        send(local.at[zz], got.at[z], s_s.at[d], r_s.at[d], at(y, zz))
    got[z] = local[z]

    for way in (0, 1):
        for k in range(1, reach):
            got_1(rest, r_b1, way, k)
        for j in range(1, reach + 1 - way):
            got_2(rest, r_b2, way, j)
    planes = ((0, slice(3, 4)), (1, slice(4, 6)), (2, slice(6, 8)))

    def cross_plane(n):
        ref = w.at[y, :, planes[n][1]]
        for d in range(1, ny):
            send(ref, ref, s_by.at[n, d], r_by.at[n, d], at(turn(y, d, ny), z))

    def got_plane(n):
        for d in range(1, ny):
            recv(w.at[turn(y, -d, ny), :, planes[n][1]], r_by.at[n, d])

    cross_plane(0)
    cross_plane(1)
    for k in range(0, taps, 4):
        piece_taps(k, min(k + 4, taps))

    for d in range(1, nz):
        zz = turn(z, -d, nz)
        recv(keeps.at[zz], r_k.at[d])
        recv(got.at[zz], r_s.at[d])
    carry = jnp.zeros((share, 128), F32)
    decay = jnp.ones((1, 128), F32)
    for zz in range(nz):
        pref[zz] = carry
        ckeep[zz] = decay
        line = keeps[zz]
        keep = line[:, 0:128]
        for lo in range(1, chans // 128):
            keep = jnp.where(lax.div(z, each) == lo, line[:, lo * 128 : lo * 128 + 128], keep)
        carry = carry * keep + got[zz].astype(F32)
        decay = decay * keep
    tot[0:share] = carry
    tot[share : share + 8] = jnp.broadcast_to(decay, (8, 128))
    for d in range(1, ny):
        send(tot, tots.at[d - 1], s_t.at[d - 1], r_t.at[d - 1], at(turn(y, d, ny), z))
    cross_plane(2)
    for d in range(1, ny):
        recv(tots.at[d - 1], r_t.at[d - 1])
    come = jnp.zeros((share, 128), F32)
    for d in range(ny - 1, 0, -1):
        new = come * tots[d - 1, share : share + 1] + tots[d - 1, 0:share]
        come = jnp.where(y >= d, new, 0.0)
    for zz in range(nz):
        back[zz] = (pref[zz] + ckeep[zz] * come).astype(BF16)
    for d in range(1, nz):
        zz = turn(z, d, nz)
        send(back.at[zz], entry.at[z], s_p.at[d], r_p.at[d], at(y, zz))
    entry[z] = back[z]

    got_plane(0)
    cs[...] = nn(frames[...], weight(3, 1)).astype(BF16)
    scores = nt(cs[...], bs[...])
    lane_head = lax.div(iota((wide, chans), 1), PS)
    acc = jnp.zeros((wide, chans), F32)
    for h in range(heads):
        only = jnp.where(lane_head == h, xs[...].astype(F32), 0.0).astype(BF16)
        acc = acc + nn((mix[h] * scores).astype(BF16), only)
    inner[...] = acc
    got_plane(1)
    zr = nn(frames[...], weight(4, 2)).astype(BF16).astype(F32)
    zs[...] = zr * jax.nn.sigmoid(zr) * gain[...]
    same = lax.div(iota((chans, chans), 0), PS) == lax.div(iota((chans, chans), 1), PS)
    block = jnp.where(same, 1.0 / PS, 0.0).astype(BF16)
    got_plane(2)

    for d in range(1, nz):
        recv(entry.at[turn(z, -d, nz)], r_p.at[d])
    come_in = jnp.concatenate(
        [entry[lo * each : (lo + 1) * each].reshape(states, 128) for lo in range(chans // 128)],
        axis=1,
    )
    ssd = inner[...] + nn(cs[...], come_in) * growth[...]
    mean = nn((ssd * ssd).astype(BF16), block)
    g = (ssd * lax.rsqrt(mean + 1e-05) * zs[...]).astype(BF16)
    ext[...] = g.astype(F32)

    cols = width // (2 * nx)
    span = rows // parts
    per = cols // depth

    def conv(lo, hi):
        acc = jnp.zeros((hi - lo, chans), F32)
        for k in range(taps):
            off = EDGE - half + k
            acc = acc + wm[k, lo:hi, :] * ext[lo + off : hi + off, :]
        act[lo:hi] = (acc * jax.nn.sigmoid(acc)).astype(BF16)

    ow = weight(6, 2)
    for p in range(parts):
        for lo in range(p * span, (p + 1) * span, 32):
            conv(lo, lo + 32)
        rows_p = act[p * span : (p + 1) * span]
        for j in range(2 * nx):
            part[p, j // 2, j % 2] = nt(rows_p, ow[j * cols : (j + 1) * cols]).astype(BF16)
        send(part.at[p, :, 1 - core], pair.at[p], s_c.at[p], r_c.at[p], {"head": 2 * x + 1 - core})
    for p in range(parts):
        recv(pair.at[p], r_c.at[p])
        for d in range(nx - 1, 0, -1):
            xx = turn(x, d, nx)
            red[p, d - 1] = (part[p, xx, core].astype(F32) + pair[p, xx].astype(F32)).astype(BF16)
            send(red.at[p, d - 1], redin.at[p, d - 1], s_x.at[p, d - 1], r_x.at[p, d - 1],
                 {"head": 2 * xx + core})
    for p in range(parts):
        res = part[p, x, core].astype(F32) + pair[p, x].astype(F32)
        for d in range(1, nx):
            recv(redin.at[p, d - 1], r_x.at[p, d - 1])
            res = res + redin[p, d - 1].astype(F32)
        out[p * span : (p + 1) * span] = res.astype(BF16)
    for copy in pending:
        copy.wait_send()


def solution(mesh):
    tms, groups = mesh.shape["tm"], mesh.shape["head"]
    ny, nz, nx = NY, tms // NY, groups // 2

    def local(frames, xw, zw, bcw, logd, gain, convw, outw, lens):
        rows, width = frames.shape
        depth, chans = xw.shape
        states = bcw.shape[1] // 2
        heads = logd.shape[0]
        taps = convw.shape[0]
        share = states * chans // (nz * 128)
        cols = width // groups
        wide = rows + 2 * EDGE
        parts = 2
        dma = pltpu.SemaphoreType.DMA
        v = pltpu.VMEM
        reach = nz // 4
        others = max(nx - 1, 1)
        scratch = [
            v((ny, nz, 8, depth, 128), BF16),
            v((wide, width), BF16),
            v((3, heads, rows), F32),
            v((1, chans), F32),
            v((taps, chans), F32),
            v((heads, wide, wide), F32),
            v((wide, chans), F32),
            v((rows, chans), F32),
            v((taps, rows, chans), F32),
            v((wide, chans), BF16),
            v((wide, states), BF16),
            v((wide, states), BF16),
            v((wide, chans), F32),
            v((wide, chans), F32),
            v((nz, share, 128), BF16),
            v((nz, share, 128), BF16),
            v((nz, 1, chans), F32),
            v((1, chans), F32),
            v((nz, share, 128), F32),
            v((nz, 1, 128), F32),
            v((share + 8, 128), F32),
            v((ny - 1, share + 8, 128), F32),
            v((nz, share, 128), BF16),
            v((nz, share, 128), BF16),
            v((wide, chans), F32),
            v((rows, chans), BF16),
            v((parts, nx, 2, rows // parts, cols), BF16),
            v((parts, nx, rows // parts, cols), BF16),
            v((parts, others, rows // parts, cols), BF16),
            v((parts, others, rows // parts, cols), BF16),
            dma((12,)),
            dma((2, reach + 1)), dma((2, reach + 1)),
            dma((2, reach + 1)), dma((2, reach + 1)),
            dma((nz, ny)), dma((nz, ny)),
            dma((2, reach + 1)), dma((2, reach + 1)),
            dma((2, reach + 1)), dma((2, reach + 1)),
            dma((3, ny)), dma((3, ny)),
            dma((2,)), dma((2,)),
            dma((2,)), dma((2,)),
            dma((nz,)), dma((nz,)),
            dma((nz,)), dma((nz,)),
            dma((ny - 1,)), dma((ny - 1,)),
            dma((nz,)), dma((nz,)),
            dma((parts,)), dma((parts,)),
            dma((parts, others)), dma((parts, others)),
        ]
        hbm = pl.BlockSpec(memory_space=pl.ANY)
        return pl.pallas_call(
            functools.partial(kernel, ny, nz, nx, parts),
            out_shape=jax.ShapeDtypeStruct((rows, cols), BF16),
            in_specs=[pl.BlockSpec(memory_space=pltpu.SMEM)] + [hbm] * 8,
            out_specs=pl.BlockSpec(memory_space=pltpu.VMEM),
            scratch_shapes=scratch,
            compiler_params=pltpu.CompilerParams(
                collective_id=0, has_side_effects=True, vmem_limit_bytes=60 * 2**20
            ),
            name="mixer",
        )(lens, frames, xw, zw, bcw, logd, gain.reshape(1, chans), convw, outw.T)

    in_specs = (
        P("tm", None), P("tm", "head"), P("tm", "head"), P("tm", None), P("head", "tm"),
        P("head"), P(None, "head"), P("head", "tm"), P(),
    )
    return jax.shard_map(
        local, mesh=mesh, in_specs=in_specs, out_specs=P("tm", "head"), check_vma=False
    )
```

time: 81.9 us -> 66.9 us (0.82)
  Pallas kernels: 78.8 us -> 65.2 us
  local copies, waits for them, and re-layouts: 2.9 us -> 1.47 us
    pallas_call x1, Pallas kernels: 78.8 us -> 65.2 us  [local(): pl.pallas_call(functools.partial(kernel, ny, nz, nx, parts), out_shape=ja...]
    unnamed x2 -> x1, local copies, waits for them, and re-layouts: 2.9 us -> 1.47 us
where the time goes in v2:
time: 66.9 us; the launch traced here: 66.7 us
  Pallas kernels  65.2 us (97%)
  local copies, waits for them, and re-layouts  1.47 us (2%)
    pallas_call x1, Pallas kernels, local(): pl.pallas_call(functools.partial(kernel, ny, nz, nx, parts), out_shape=ja...  65.2 us
    unnamed x1, local copies, waits for them, and re-layouts  1.47 us

profile of v2, /device:TPU:1, one launch (start us, length us, event | category | flops | bytes accessed | tf_op | source)
XLA Modules:
  0.0 66.7 jit_solution(2266322261574652513)
XLA Ops:
  0.0 65.2 %mixer.1 = bf16[256,128]{1,0:T(8,128)(2,1)} custom-call(s32[8]{0:T(128)} %lens.1, bf16[256,1024]{1,0:T(8,128)(2,1)} %frames_in.1, bf16[16,256]{1,0:T(8,128)(2,1)} %xw.1, bf16[16,256]{1,0:T(8,128)(2,1)} %zw.1, bf16[16,256]{1,0:T(8,128)(2,1)} %bcw.1, f32[4,256]{1,0:T(4,128)} %logd_in.1, f32[1,256]{1,0:T(1,128)} %bitcast.3, f32[31,256]{1,0:T(8,128)} %convw_in.1, ...), custom_call_target="tpu_custom_call" | custom-call | tf_op jit(solution)/shard_map/mixer/pallas_call | solution.py:432
  65.3 1.5 %copy.11 = bf16[256,128]{1,0:T(8,128)(2,1)} copy(bf16[256,128]{1,0:T(8,128)(2,1)} %mixer.1) | data formatting | bytes 131072

commit v3 on v2

--- a/solution.py
+++ b/solution.py
@@ -34,11 +34,11 @@
 
 def kernel(
     ny, nz, nx, parts,
-    lens, frames_in, xw, zw, bcw, logd_in, gain_in, convw_in, outw, out,
-    w, frames, logd, gain, convw, mix, growth, tail, wm, xs, bs, cs, inner, zs,
+    lens_in, frames_in, xw, zw, bcw, logd_in, gain_in, convw_in, outw, out,
+    lens, w, frames, logd, gain, convw, mix, growth, tail, wm, xs, bs, cs, inner, zs,
     local, got, keeps, keep_own, pref, ckeep, tot, tots, back, entry, ext, act,
     part, pair, red, redin,
-    s_loc, s_a1, r_a1, s_a2, r_a2, s_ay, r_ay, s_b1, r_b1, s_b2, r_b2, s_by, r_by,
+    s_loc, s_a1, r_a1, s_a2, r_a2, s_ay, r_ay, s_b, r_b, s_by, r_by,
     s_f, r_f, s_l, r_l, s_k, r_k, s_s, r_s, s_t, r_t, s_p, r_p, s_c, r_c, s_x, r_x,
 ):
     me, hd = lax.axis_index("tm"), lax.axis_index("head")
@@ -52,7 +52,9 @@
     states = bcw.shape[1] // 2
     taps = convw_in.shape[0]
     half = (taps - 1) // 2
-    reach = nz // 4
+    reach = max(nz // 4, 1)
+    hop = max(nz // 8, 1)
+    stages = nz // 2 // hop
     base = me * rows
     first = base - EDGE
 
@@ -71,6 +73,13 @@
         )
         copy.start()
         pending.append(copy)
+
+    done = [0]
+
+    def drain(upto):
+        while done[0] < upto:
+            pending[done[0]].wait_send()
+            done[0] += 1
 
     def recv(dst, rsem):
         pltpu.make_async_copy(dst, dst, rsem).wait()
@@ -93,6 +102,7 @@
     own.append(pltpu.make_async_copy(frames_in, frames.at[EDGE : EDGE + rows], s_loc.at[9]))
     own.append(pltpu.make_async_copy(gain_in, gain, s_loc.at[10]))
     own.append(pltpu.make_async_copy(convw_in, convw, s_loc.at[11]))
+    own.append(pltpu.make_async_copy(lens_in, lens, s_loc.at[12]))
     for copy in own:
         copy.start()
     for copy in own:
@@ -101,16 +111,16 @@
 
     crit, rest = slice(0, 3), slice(3, 8)
 
-    def stage_1(cut, ssem, rsem):
+    def stage_1(cut, ssem, rsem, reach):
         ref = w.at[y, z, cut]
         for k in range(reach, 0, -1):
             for way, s in ((0, 1), (1, -1)):
                 send(ref, ref, ssem.at[way, k], rsem.at[way, k], at(y, turn(z, s * k, nz)))
 
-    def stage_2(cut, ssem, rsem, way):
+    def stage_2(cut, ssem, rsem, way, reach):
         s = 1 - 2 * way
         ref = w.at[y, turn(z, -s * reach, nz), cut]
-        for j in range(reach - way, 0, -1):
+        for j in range(nz // 2 - reach - way, 0, -1):
             send(ref, ref, ssem.at[way, j], rsem.at[way, j], at(y, turn(z, s * j, nz)))
 
     def cross(off):
@@ -119,14 +129,46 @@
         for d in range(1, ny):
             send(ref, ref, s_ay.at[off % nz, d], r_ay.at[off % nz, d], at(turn(y, d, ny), z))
 
+    def rest_ref(way, dist):
+        return w.at[y, turn(z, dist if way else -dist, nz), rest]
+
+    def rest_stage(s):
+        src = (s - 1) * hop
+        for j in range(hop, 0, -1):
+            for way in (0, 1):
+                dist = src + j
+                if dist < nz // 2 or way == 0:
+                    ref = rest_ref(way, src)
+                    send(ref, ref, s_b.at[way, dist], r_b.at[way, dist],
+                         at(y, turn(z, -j if way else j, nz)))
+
+    def rest_cross(off):
+        ref = w.at[y, turn(z, -off, nz), rest]
+        for d in range(1, ny):
+            send(ref, ref, s_by.at[off % nz, d], r_by.at[off % nz, d], at(turn(y, d, ny), z))
+
+    def rest_step(s):
+        if s > stages:
+            return
+        for j in range(hop, 0, -1):
+            dist = (s - 1) * hop + j
+            for way in (0, 1):
+                if dist < nz // 2 or way == 0:
+                    recv(rest_ref(way, dist), r_b.at[way, dist])
+            if j == hop and s < stages:
+                rest_stage(s + 1)
+            for way in (0, 1):
+                if dist < nz // 2 or way == 0:
+                    rest_cross(-dist if way else dist)
+
     def got_1(cut, rsem, way, k):
         recv(w.at[y, turn(z, k if way else -k, nz), cut], rsem.at[way, k])
 
-    def got_2(cut, rsem, way, j):
+    def got_2(cut, rsem, way, j, reach):
         far = reach + j
         recv(w.at[y, turn(z, far if way else -far, nz), cut], rsem.at[way, j])
 
-    stage_1(crit, s_a1, r_a1)
+    stage_1(crit, s_a1, r_a1, reach)
     cross(0)
     for i, d in enumerate((1, -1)):
         send(logd.at[1], logd.at[1 - d], s_l.at[i], r_l.at[i], {"tm": turn(me, d, tms)})
@@ -195,35 +237,33 @@
 
     for way in (0, 1):
         got_1(crit, r_a1, way, reach)
-        stage_2(crit, s_a2, r_a2, way)
-    stage_1(rest, s_b1, r_b1)
-    for k in range(reach, 0, -1):
+        stage_2(crit, s_a2, r_a2, way, reach)
+        cross(reach if way == 0 else -reach)
+    rest_stage(1)
+    for k in range(reach - 1, 0, -1):
         for way in (0, 1):
-            if k < reach:
-                got_1(crit, r_a1, way, k)
+            got_1(crit, r_a1, way, k)
             cross(k if way == 0 else -k)
     recv(logd.at[0], r_l.at[0])
     recv(logd.at[2], r_l.at[1])
     piece_cumul()
-    for j in range(1, reach + 1):
+    for j in range(1, nz // 2 - reach + 1):
         for way in (0, 1):
-            if j <= reach - way:
-                got_2(crit, r_a2, way, j)
+            if j <= nz // 2 - reach - way:
+                got_2(crit, r_a2, way, j, reach)
                 cross(reach + j if way == 0 else -(reach + j))
-    for way in (0, 1):
-        got_1(rest, r_b1, way, reach)
-        stage_2(rest, s_b2, r_b2, way)
+    rest_cross(0)
+    rest_step(1)
     keeps[z] = keep_own[...]
     for d in range(1, nz):
         send(keep_own, keeps.at[z], s_k.at[d], r_k.at[d], at(y, turn(z, d, nz)))
     for h in range(heads):
         piece_mix(h)
+    recv(frames.at[0:EDGE], r_f.at[0])
+    recv(frames.at[rows + EDGE : wide], r_f.at[1])
     for off in range(nz):
         for d in range(1, ny):
             recv(w.at[turn(y, -d, ny), turn(z, -off, nz), crit], r_ay.at[off, d])
-
-    recv(frames.at[0:EDGE], r_f.at[0])
-    recv(frames.at[rows + EDGE : wide], r_f.at[1])
 
     def weight(lo, count):
         return jnp.concatenate(
@@ -241,35 +281,23 @@
         local[lo * each : (lo + 1) * each] = state[:, lo * 128 : lo * 128 + 128].reshape(
             each, share, 128
         )
+    mark = len(pending)
     for d in range(1, nz):
         zz = turn(z, d, nz)
         send(local.at[zz], got.at[z], s_s.at[d], r_s.at[d], at(y, zz))
     got[z] = local[z]
 
-    for way in (0, 1):
-        for k in range(1, reach):
-            got_1(rest, r_b1, way, k)
-        for j in range(1, reach + 1 - way):
-            got_2(rest, r_b2, way, j)
-    planes = ((0, slice(3, 4)), (1, slice(4, 6)), (2, slice(6, 8)))
-
-    def cross_plane(n):
-        ref = w.at[y, :, planes[n][1]]
-        for d in range(1, ny):
-            send(ref, ref, s_by.at[n, d], r_by.at[n, d], at(turn(y, d, ny), z))
-
-    def got_plane(n):
-        for d in range(1, ny):
-            recv(w.at[turn(y, -d, ny), :, planes[n][1]], r_by.at[n, d])
-
-    cross_plane(0)
-    cross_plane(1)
+    rest_step(2)
     for k in range(0, taps, 4):
         piece_taps(k, min(k + 4, taps))
+    rest_step(3)
+
+    for d in range(1, nz):
+        recv(keeps.at[turn(z, -d, nz)], r_k.at[d])
+    drain(mark)
 
     for d in range(1, nz):
         zz = turn(z, -d, nz)
-        recv(keeps.at[zz], r_k.at[d])
         recv(got.at[zz], r_s.at[d])
     carry = jnp.zeros((share, 128), F32)
     decay = jnp.ones((1, 128), F32)
@@ -286,7 +314,7 @@
     tot[share : share + 8] = jnp.broadcast_to(decay, (8, 128))
     for d in range(1, ny):
         send(tot, tots.at[d - 1], s_t.at[d - 1], r_t.at[d - 1], at(turn(y, d, ny), z))
-    cross_plane(2)
+    rest_step(4)
     for d in range(1, ny):
         recv(tots.at[d - 1], r_t.at[d - 1])
     come = jnp.zeros((share, 128), F32)
@@ -295,12 +323,15 @@
         come = jnp.where(y >= d, new, 0.0)
     for zz in range(nz):
         back[zz] = (pref[zz] + ckeep[zz] * come).astype(BF16)
+    mark = len(pending)
     for d in range(1, nz):
         zz = turn(z, d, nz)
         send(back.at[zz], entry.at[z], s_p.at[d], r_p.at[d], at(y, zz))
     entry[z] = back[z]
 
-    got_plane(0)
+    for off in range(nz):
+        for d in range(1, ny):
+            recv(w.at[turn(y, -d, ny), turn(z, -off, nz), rest], r_by.at[off, d])
     cs[...] = nn(frames[...], weight(3, 1)).astype(BF16)
     scores = nt(cs[...], bs[...])
     lane_head = lax.div(iota((wide, chans), 1), PS)
@@ -309,12 +340,11 @@
         only = jnp.where(lane_head == h, xs[...].astype(F32), 0.0).astype(BF16)
         acc = acc + nn((mix[h] * scores).astype(BF16), only)
     inner[...] = acc
-    got_plane(1)
     zr = nn(frames[...], weight(4, 2)).astype(BF16).astype(F32)
     zs[...] = zr * jax.nn.sigmoid(zr) * gain[...]
     same = lax.div(iota((chans, chans), 0), PS) == lax.div(iota((chans, chans), 1), PS)
     block = jnp.where(same, 1.0 / PS, 0.0).astype(BF16)
-    got_plane(2)
+    drain(mark)
 
     for d in range(1, nz):
         recv(entry.at[turn(z, -d, nz)], r_p.at[d])
@@ -359,8 +389,7 @@
             recv(redin.at[p, d - 1], r_x.at[p, d - 1])
             res = res + redin[p, d - 1].astype(F32)
         out[p * span : (p + 1) * span] = res.astype(BF16)
-    for copy in pending:
-        copy.wait_send()
+    drain(len(pending))
 
 
 def solution(mesh):
@@ -379,9 +408,9 @@
         parts = 2
         dma = pltpu.SemaphoreType.DMA
         v = pltpu.VMEM
-        reach = nz // 4
         others = max(nx - 1, 1)
         scratch = [
+            pltpu.SMEM(lens.shape, jnp.int32),
             v((ny, nz, 8, depth, 128), BF16),
             v((wide, width), BF16),
             v((3, heads, rows), F32),
@@ -412,13 +441,12 @@
             v((parts, nx, rows // parts, cols), BF16),
             v((parts, others, rows // parts, cols), BF16),
             v((parts, others, rows // parts, cols), BF16),
-            dma((12,)),
-            dma((2, reach + 1)), dma((2, reach + 1)),
-            dma((2, reach + 1)), dma((2, reach + 1)),
+            dma((13,)),
+            dma((2, nz // 2 + 1)), dma((2, nz // 2 + 1)),
+            dma((2, nz // 2 + 1)), dma((2, nz // 2 + 1)),
             dma((nz, ny)), dma((nz, ny)),
-            dma((2, reach + 1)), dma((2, reach + 1)),
-            dma((2, reach + 1)), dma((2, reach + 1)),
-            dma((3, ny)), dma((3, ny)),
+            dma((2, nz // 2 + 1)), dma((2, nz // 2 + 1)),
+            dma((nz, ny)), dma((nz, ny)),
             dma((2,)), dma((2,)),
             dma((2,)), dma((2,)),
             dma((nz,)), dma((nz,)),
@@ -432,7 +460,7 @@
         return pl.pallas_call(
             functools.partial(kernel, ny, nz, nx, parts),
             out_shape=jax.ShapeDtypeStruct((rows, cols), BF16),
-            in_specs=[pl.BlockSpec(memory_space=pltpu.SMEM)] + [hbm] * 8,
+            in_specs=[hbm] * 9,
             out_specs=pl.BlockSpec(memory_space=pltpu.VMEM),
             scratch_shapes=scratch,
             compiler_params=pltpu.CompilerParams(

time: 66.9 us -> 65.2 us (0.975)
  Pallas kernels: 65.2 us -> 63.5 us
    pallas_call x1, Pallas kernels: 65.2 us -> 63.5 us  [local(): pl.pallas_call(functools.partial(kernel, ny, nz, nx, parts), out_shape=ja...]
where the time goes in v3:
time: 65.2 us; the launch traced here: 65 us
  Pallas kernels  63.5 us (97%)
  local copies, waits for them, and re-layouts  1.47 us (2%)
    pallas_call x1, Pallas kernels, local(): pl.pallas_call(functools.partial(kernel, ny, nz, nx, parts), out_shape=ja...  63.5 us
    unnamed x1, local copies, waits for them, and re-layouts  1.47 us

profile of v3, /device:TPU:1, one launch (start us, length us, event | category | flops | bytes accessed | tf_op | source)
XLA Modules:
  0.0 65.0 jit_solution(7560141888959207748)
XLA Ops:
  0.0 63.5 %mixer.1 = bf16[256,128]{1,0:T(8,128)(2,1)} custom-call(s32[8]{0:T(128)} %lens_in.1, bf16[256,1024]{1,0:T(8,128)(2,1)} %frames_in.1, bf16[16,256]{1,0:T(8,128)(2,1)} %xw.1, bf16[16,256]{1,0:T(8,128)(2,1)} %zw.1, bf16[16,256]{1,0:T(8,128)(2,1)} %bcw.1, f32[4,256]{1,0:T(4,128)} %logd_in.1, f32[1,256]{1,0:T(1,128)} %bitcast.3, f32[31,256]{1,0:T(8,128)} %convw_in.1, ...), custom_call_target="tpu_custom_call" | custom-call | tf_op jit(solution)/shard_map/mixer/pallas_call | solution.py:460
  63.5 1.5 %copy.11 = bf16[256,128]{1,0:T(8,128)(2,1)} copy(bf16[256,128]{1,0:T(8,128)(2,1)} %mixer.1) | data formatting | bytes 131072

commit v4 on v3

--- a/solution.py
+++ b/solution.py
@@ -405,7 +405,7 @@
         share = states * chans // (nz * 128)
         cols = width // groups
         wide = rows + 2 * EDGE
-        parts = 2
+        parts = 4
         dma = pltpu.SemaphoreType.DMA
         v = pltpu.VMEM
         others = max(nx - 1, 1)
@@ -456,7 +456,7 @@
             dma((parts,)), dma((parts,)),
             dma((parts, others)), dma((parts, others)),
         ]
-        hbm = pl.BlockSpec(memory_space=pl.ANY)
+        hbm = pl.BlockSpec(memory_space=pltpu.HBM)
         return pl.pallas_call(
             functools.partial(kernel, ny, nz, nx, parts),
             out_shape=jax.ShapeDtypeStruct((rows, cols), BF16),
@@ -464,10 +464,13 @@
             out_specs=pl.BlockSpec(memory_space=pltpu.VMEM),
             scratch_shapes=scratch,
             compiler_params=pltpu.CompilerParams(
-                collective_id=0, has_side_effects=True, vmem_limit_bytes=60 * 2**20
+                collective_id=0, has_side_effects=True, vmem_limit_bytes=28 * 2**20
             ),
             name="mixer",
-        )(lens, frames, xw, zw, bcw, logd, gain.reshape(1, chans), convw, outw.T)
+        )(*[
+            pltpu.with_memory_space_constraint(v, pltpu.HBM)
+            for v in (lens, frames, xw, zw, bcw, logd, gain.reshape(1, chans), convw, outw.T)
+        ])
 
     in_specs = (
         P("tm", None), P("tm", "head"), P("tm", "head"), P("tm", None), P("head", "tm"),

time: 65.2 us -> 63.1 us (0.968)
  Pallas kernels: 63.5 us -> 62.3 us
  local copies, waits for them, and re-layouts: 1.47 us -> 0.63 us
    pallas_call x1, Pallas kernels: 63.5 us -> 62.3 us  [local(): pl.pallas_call(functools.partial(kernel, ny, nz, nx, parts), out_shape=ja...]
    unnamed x1, local copies, waits for them, and re-layouts: 1.47 us -> 0.63 us
where the time goes in v4:
time: 63.1 us; the launch traced here: 62.9 us
  Pallas kernels  62.3 us (99%)
    pallas_call x1, Pallas kernels, local(): pl.pallas_call(functools.partial(kernel, ny, nz, nx, parts), out_shape=ja...  62.3 us

profile of v4, /device:TPU:1, one launch (start us, length us, event | category | flops | bytes accessed | tf_op | source)
XLA Modules:
  0.0 62.9 jit_solution(5593978391233713530)
XLA Ops:
  0.0 62.3 %mixer.1 = bf16[256,128]{1,0:T(8,128)(2,1)S(1)} custom-call(s32[8]{0:T(128)} %lens_in.1, bf16[256,1024]{1,0:T(8,128)(2,1)} %frames_in.1, bf16[16,256]{1,0:T(8,128)(2,1)} %xw.1, bf16[16,256]{1,0:T(8,128)(2,1)} %zw.1, bf16[16,256]{1,0:T(8,128)(2,1)} %bcw.1, f32[4,256]{1,0:T(4,128)} %logd_in.1, f32[1,256]{1,0:T(1,128)} %bitcast.3, f32[31,256]{1,0:T(8,128)} %convw_in.1, ...), custom_call_target="tpu_custom_call" | custom-call | tf_op jit(solution)/shard_map/mixer/pallas_call | solution.py:460
  62.3 0.6 %copy.11 = bf16[256,128]{1,0:T(8,128)(2,1)} copy(bf16[256,128]{1,0:T(8,128)(2,1)S(1)} %mixer.1) | data formatting | bytes 131072

commit v5 on v4

--- a/solution.py
+++ b/solution.py
@@ -64,6 +64,9 @@
     def turn(a, d, n):
         return lax.rem(a + d + n, n)
 
+    def ring(n):
+        return sorted(range(1, n), key=lambda d: (-min(d, n - d), d))
+
     pending = []
 
     def send(src, dst, ssem, rsem, dev):
@@ -105,7 +108,7 @@
     own.append(pltpu.make_async_copy(lens_in, lens, s_loc.at[12]))
     for copy in own:
         copy.start()
-    for copy in own:
+    for copy in own[0:3]:
         copy.wait()
     pl.semaphore_wait(barrier, len(greet))
 
@@ -126,7 +129,7 @@
     def cross(off):
         zz = turn(z, -off, nz)
         ref = w.at[y, zz, crit]
-        for d in range(1, ny):
+        for d in ring(ny):
             send(ref, ref, s_ay.at[off % nz, d], r_ay.at[off % nz, d], at(turn(y, d, ny), z))
 
     def rest_ref(way, dist):
@@ -144,7 +147,7 @@
 
     def rest_cross(off):
         ref = w.at[y, turn(z, -off, nz), rest]
-        for d in range(1, ny):
+        for d in ring(ny):
             send(ref, ref, s_by.at[off % nz, d], r_by.at[off % nz, d], at(turn(y, d, ny), z))
 
     def rest_step(s):
@@ -170,6 +173,8 @@
 
     stage_1(crit, s_a1, r_a1, reach)
     cross(0)
+    for copy in own[3:]:
+        copy.wait()
     for i, d in enumerate((1, -1)):
         send(logd.at[1], logd.at[1 - d], s_l.at[i], r_l.at[i], {"tm": turn(me, d, tms)})
     send(frames.at[rows : rows + EDGE], frames.at[0:EDGE],
@@ -255,7 +260,7 @@
     rest_cross(0)
     rest_step(1)
     keeps[z] = keep_own[...]
-    for d in range(1, nz):
+    for d in ring(nz):
         send(keep_own, keeps.at[z], s_k.at[d], r_k.at[d], at(y, turn(z, d, nz)))
     for h in range(heads):
         piece_mix(h)
@@ -282,7 +287,7 @@
             each, share, 128
         )
     mark = len(pending)
-    for d in range(1, nz):
+    for d in ring(nz):
         zz = turn(z, d, nz)
         send(local.at[zz], got.at[z], s_s.at[d], r_s.at[d], at(y, zz))
     got[z] = local[z]
@@ -312,7 +317,7 @@
         decay = decay * keep
     tot[0:share] = carry
     tot[share : share + 8] = jnp.broadcast_to(decay, (8, 128))
-    for d in range(1, ny):
+    for d in ring(ny):
         send(tot, tots.at[d - 1], s_t.at[d - 1], r_t.at[d - 1], at(turn(y, d, ny), z))
     rest_step(4)
     for d in range(1, ny):
@@ -324,7 +329,7 @@
     for zz in range(nz):
         back[zz] = (pref[zz] + ckeep[zz] * come).astype(BF16)
     mark = len(pending)
-    for d in range(1, nz):
+    for d in ring(nz):
         zz = turn(z, d, nz)
         send(back.at[zz], entry.at[z], s_p.at[d], r_p.at[d], at(y, zz))
     entry[z] = back[z]
@@ -378,7 +383,7 @@
         send(part.at[p, :, 1 - core], pair.at[p], s_c.at[p], r_c.at[p], {"head": 2 * x + 1 - core})
     for p in range(parts):
         recv(pair.at[p], r_c.at[p])
-        for d in range(nx - 1, 0, -1):
+        for d in ring(nx):
             xx = turn(x, d, nx)
             red[p, d - 1] = (part[p, xx, core].astype(F32) + pair[p, xx].astype(F32)).astype(BF16)
             send(red.at[p, d - 1], redin.at[p, d - 1], s_x.at[p, d - 1], r_x.at[p, d - 1],

time: 63.1 us -> 62.5 us (level)
  no operation moved by 1% of the time
where the time goes in v5:
time: 62.5 us; the launch traced here: 62.4 us
  Pallas kernels  61.7 us (99%)
  local copies, waits for them, and re-layouts  0.63 us (1%)
    pallas_call x1, Pallas kernels, local(): pl.pallas_call(functools.partial(kernel, ny, nz, nx, parts), out_shape=ja...  61.7 us

profile of v5, /device:TPU:1, one launch (start us, length us, event | category | flops | bytes accessed | tf_op | source)
XLA Modules:
  0.0 62.4 jit_solution(12703431436605404590)
XLA Ops:
  0.0 61.7 %mixer.1 = bf16[256,128]{1,0:T(8,128)(2,1)S(1)} custom-call(s32[8]{0:T(128)} %lens_in.1, bf16[256,1024]{1,0:T(8,128)(2,1)} %frames_in.1, bf16[16,256]{1,0:T(8,128)(2,1)} %xw.1, bf16[16,256]{1,0:T(8,128)(2,1)} %zw.1, bf16[16,256]{1,0:T(8,128)(2,1)} %bcw.1, f32[4,256]{1,0:T(4,128)} %logd_in.1, f32[1,256]{1,0:T(1,128)} %bitcast.3, f32[31,256]{1,0:T(8,128)} %convw_in.1, ...), custom_call_target="tpu_custom_call" | custom-call | tf_op jit(solution)/shard_map/mixer/pallas_call | solution.py:465
  61.7 0.6 %copy.11 = bf16[256,128]{1,0:T(8,128)(2,1)} copy(bf16[256,128]{1,0:T(8,128)(2,1)S(1)} %mixer.1) | data formatting | bytes 131072

commit v6 on v5

--- a/solution.py
+++ b/solution.py
@@ -181,6 +181,8 @@
          s_f.at[0], r_f.at[0], {"tm": turn(me, 1, tms)})
     send(frames.at[EDGE : 2 * EDGE], frames.at[rows + EDGE : wide],
          s_f.at[1], r_f.at[1], {"tm": turn(me, -1, tms)})
+    rest_stage(1)
+    rest_cross(0)
 
     ends = []
     total = jnp.int32(0)
@@ -244,7 +246,6 @@
         got_1(crit, r_a1, way, reach)
         stage_2(crit, s_a2, r_a2, way, reach)
         cross(reach if way == 0 else -reach)
-    rest_stage(1)
     for k in range(reach - 1, 0, -1):
         for way in (0, 1):
             got_1(crit, r_a1, way, k)
@@ -257,7 +258,6 @@
             if j <= nz // 2 - reach - way:
                 got_2(crit, r_a2, way, j, reach)
                 cross(reach + j if way == 0 else -(reach + j))
-    rest_cross(0)
     rest_step(1)
     keeps[z] = keep_own[...]
     for d in ring(nz):

time: 62.5 us -> 62.6 us (level)
  no operation moved by 1% of the time
where the time goes in v6:
time: 62.6 us; the launch traced here: 62.5 us
  Pallas kernels  61.9 us (99%)
  local copies, waits for them, and re-layouts  0.63 us (1%)
    pallas_call x1, Pallas kernels, local(): pl.pallas_call(functools.partial(kernel, ny, nz, nx, parts), out_shape=ja...  61.9 us

profile of v6, /device:TPU:1, one launch (start us, length us, event | category | flops | bytes accessed | tf_op | source)
XLA Modules:
  0.0 62.5 jit_solution(8217724081279677875)
XLA Ops:
  0.0 61.9 %mixer.1 = bf16[256,128]{1,0:T(8,128)(2,1)S(1)} custom-call(s32[8]{0:T(128)} %lens_in.1, bf16[256,1024]{1,0:T(8,128)(2,1)} %frames_in.1, bf16[16,256]{1,0:T(8,128)(2,1)} %xw.1, bf16[16,256]{1,0:T(8,128)(2,1)} %zw.1, bf16[16,256]{1,0:T(8,128)(2,1)} %bcw.1, f32[4,256]{1,0:T(4,128)} %logd_in.1, f32[1,256]{1,0:T(1,128)} %bitcast.3, f32[31,256]{1,0:T(8,128)} %convw_in.1, ...), custom_call_target="tpu_custom_call" | custom-call | tf_op jit(solution)/shard_map/mixer/pallas_call | solution.py:465
  61.9 0.6 %copy.11 = bf16[256,128]{1,0:T(8,128)(2,1)} copy(bf16[256,128]{1,0:T(8,128)(2,1)S(1)} %mixer.1) | data formatting | bytes 131072

commit v7 on v5

--- a/solution.py
+++ b/solution.py
@@ -410,7 +410,7 @@
         share = states * chans // (nz * 128)
         cols = width // groups
         wide = rows + 2 * EDGE
-        parts = 4
+        parts = 8
         dma = pltpu.SemaphoreType.DMA
         v = pltpu.VMEM
         others = max(nx - 1, 1)

time: 62.5 us -> 63.2 us (1.011)
  Pallas kernels: 61.7 us -> 62.5 us
    pallas_call x1, Pallas kernels: 61.7 us -> 62.5 us  [local(): pl.pallas_call(functools.partial(kernel, ny, nz, nx, parts), out_shape=ja...]
where the time goes in v7:
time: 63.2 us; the launch traced here: 63.1 us
  Pallas kernels  62.5 us (99%)
    pallas_call x1, Pallas kernels, local(): pl.pallas_call(functools.partial(kernel, ny, nz, nx, parts), out_shape=ja...  62.5 us

profile of v7, /device:TPU:1, one launch (start us, length us, event | category | flops | bytes accessed | tf_op | source)
XLA Modules:
  0.0 63.1 jit_solution(6491332847464571148)
XLA Ops:
  0.0 62.5 %mixer.1 = bf16[256,128]{1,0:T(8,128)(2,1)S(1)} custom-call(s32[8]{0:T(128)} %lens_in.1, bf16[256,1024]{1,0:T(8,128)(2,1)} %frames_in.1, bf16[16,256]{1,0:T(8,128)(2,1)} %xw.1, bf16[16,256]{1,0:T(8,128)(2,1)} %zw.1, bf16[16,256]{1,0:T(8,128)(2,1)} %bcw.1, f32[4,256]{1,0:T(4,128)} %logd_in.1, f32[1,256]{1,0:T(1,128)} %bitcast.3, f32[31,256]{1,0:T(8,128)} %convw_in.1, ...), custom_call_target="tpu_custom_call" | custom-call | tf_op jit(solution)/shard_map/mixer/pallas_call | solution.py:465
  62.5 0.6 %copy.11 = bf16[256,128]{1,0:T(8,128)(2,1)} copy(bf16[256,128]{1,0:T(8,128)(2,1)S(1)} %mixer.1) | data formatting | bytes 131072
